TPU v7x, 32 devices: a whole 2x2x4 slice. The times are simulated.
32 devices in a mesh: harm: 8 (over z, x), slab: 4 (over y, core).
Axes of the slice: x: 2, y: 2, z: 4, core: 2. Of those that a mesh axis runs over, the one named last changes fastest.
Arguments:
- harmonics: float32 [8, 2, 5, 8, 2048], P('harm', None, None, 'slab'), may hold values from -4 to 4
- mean_flow: float32 [5, 8, 2048], P(None, 'slab'), may hold values from 0.5 to 13.5
- freq_index: int32 [8], P('harm'), may hold values from 1 to 8
- wall_mask: int32 [8, 2048], P('slab'), may hold values 0 or 1
- jacobian_x: float32 [5, 5], replicated, may hold values from -2.5 to 2.5
- jacobian_y: float32 [5, 5], replicated, may hold values from -2.5 to 2.5
Outputs:
- mean_next: float32 [5, 8, 2048], P(None, 'slab')
- harmonics_next: float32 [8, 2, 5, 8, 2048], P('harm', None, None, 'slab')
All inputs are finite; a program needn't handle non-finite values. No bound on the sum of `wall_mask` on one device may be relied on, other than what follows from the above.
Results may differ from a plain program's by a relative error of at most 0.00018.
Values sent between devices are 32-bit elements; how exact they have to be, the bound alone decides.
A program may use at most 64 MiB of HBM per device.

v0:
```python
import jax
import jax.numpy as jnp
from jax import lax
from jax.sharding import PartitionSpec as P

NZ = 64


EPS_FOURTH = 0.05
COURANT = 0.9
OMEGA_BASE = 0.25
WALL_RATE = 2.0
HUB_RADIUS = 0.5
SECTION_RATES = (0.25, 1.0 / 3.0, 0.5, 1.0)
STRESS_PAIRS = ((1, 1), (1, 2), (1, 3), (2, 2), (2, 3), (3, 3), (4, 1), (4, 2), (4, 3))


def with_halo(cells, sides, width):
    for axis, dim in sides:
        count = lax.axis_size(axis)
        ends = count - 1
        head = lax.slice_in_dim(cells, 0, width, axis=dim)
        tail = lax.slice_in_dim(cells, cells.shape[dim] - width, cells.shape[dim], axis=dim)
        cells = jnp.concatenate(
            [
                lax.ppermute(tail, axis, [(i, (i + 1) % count) for i in range(ends)]),
                cells,
                lax.ppermute(head, axis, [((i + 1) % count, i) for i in range(ends)]),
            ],
            axis=dim,
        )
    return cells


def apply_matrix(matrix, values):
    return jnp.einsum("ab,...bxp->...axp", matrix, values, precision=lax.Precision.HIGHEST)


def diff_across(values):
    return (jnp.roll(values, -NZ, axis=-1) - jnp.roll(values, NZ, axis=-1)) * 0.5


def fourth_across(values):
    return (
        jnp.roll(values, -2 * NZ, axis=-1)
        - 4.0 * jnp.roll(values, -NZ, axis=-1)
        + 6.0 * values
        - 4.0 * jnp.roll(values, NZ, axis=-1)
        + jnp.roll(values, 2 * NZ, axis=-1)
    )


def diff_along(padded):
    return (padded[..., 3:-1, :] - padded[..., 1:-3, :]) * 0.5


def fourth_along(padded):
    return (
        padded[..., 4:, :]
        - 4.0 * padded[..., 3:-1, :]
        + 6.0 * padded[..., 2:-2, :]
        - 4.0 * padded[..., 1:-3, :]
        + padded[..., :-4, :]
    )


def harmonic_residual(harm_pad, momentum_pad, omegas, wall_cells, jac_x, jac_y):
    center = harm_pad[..., 2:-2, :]
    flux_x = apply_matrix(jac_x, harm_pad * momentum_pad)
    flux_y = apply_matrix(jac_y, center)
    rotation = jnp.stack([center[..., 1, :, :, :], -center[..., 0, :, :, :]], axis=-4) * omegas
    return (
        rotation
        - diff_along(flux_x)
        - diff_across(flux_y)
        - EPS_FOURTH * (fourth_along(harm_pad) + fourth_across(center))
        - WALL_RATE * wall_cells * center
    )


def stresses(values):
    fields = []
    for first, second in STRESS_PAIRS:
        product = values[..., first, :, :] * values[..., second, :, :]
        fields.append(0.5 * jnp.sum(product, axis=tuple(range(product.ndim - 2))))
    return jnp.stack(fields, axis=0)


def forcing(stress_pad, radius):
    center = stress_pad[:, 1:-1, :]
    grad_x = (stress_pad[:, 2:, :] - stress_pad[:, :-2, :]) * 0.5
    grad_y = diff_across(center)
    first = -grad_x[0] - grad_y[1]
    second = -grad_x[1] - grad_y[3] - 2.0 * center[4] / radius
    third = -grad_x[2] - grad_y[4] + (center[3] - center[5]) / radius
    fourth = -grad_x[6] - grad_y[7] - center[8] / radius
    return jnp.stack([first, second, third, fourth], axis=0)


def mean_residual(mean_pad, forcing_terms, jac_x, jac_y):
    center = mean_pad[:, 2:-2, :]
    residual = (
        -diff_along(apply_matrix(jac_x, mean_pad))
        - diff_across(apply_matrix(jac_y, center))
        - EPS_FOURTH * (fourth_along(mean_pad) + fourth_across(center))
    )
    zeros_row = jnp.zeros_like(forcing_terms[:1])
    return residual + jnp.concatenate([zeros_row, forcing_terms], axis=0)


def shards(harmonics, mean_flow, freq_index, wall_mask, jacobian_x, jacobian_y):
    owned = harmonics.shape[0]
    slab_cells = mean_flow.shape[1]
    plane_count = mean_flow.shape[2]
    radius = HUB_RADIUS + ((jnp.arange(plane_count) % NZ).astype(jnp.float32) + 0.5) / NZ
    wall_cells = wall_mask.astype(jnp.float32)
    omegas = (OMEGA_BASE * freq_index.astype(jnp.float32)).reshape(owned, 1, 1, 1, 1)
    speed_total = lax.psum(jnp.sum(mean_flow[1] * mean_flow[1]), "slab")
    cell_count = slab_cells * lax.axis_size("slab") * plane_count
    time_step = COURANT / (1.0 + jnp.sqrt(speed_total / cell_count))
    harm_now, mean_now = (harmonics, mean_flow)
    for section_rate in SECTION_RATES:
        stacked = jnp.concatenate(
            [harm_now.reshape(owned * 2, 5, slab_cells, plane_count), mean_now[None]], axis=0
        )
        padded = with_halo(stacked, (("slab", 2),), 2)
        harm_pad = padded[: 2 * owned].reshape(owned, 2, 5, slab_cells + 4, plane_count)
        mean_pad = padded[2 * owned]
        harm_res = harmonic_residual(
            harm_pad, mean_pad[1], omegas, wall_cells, jacobian_x, jacobian_y
        )
        partial_terms = forcing(stresses(harm_pad[..., 1:-1, :]), radius)
        forcing_terms = lax.psum(partial_terms, "harm")
        mean_res = mean_residual(mean_pad, forcing_terms, jacobian_x, jacobian_y)
        harm_now = harmonics + section_rate * time_step * harm_res
        mean_now = mean_flow + section_rate * time_step * mean_res
    return (mean_now, harm_now)


def solution(mesh):
    placed = (
        P("harm", None, None, "slab", None),
        P(None, "slab", None),
        P("harm"),
        P("slab", None),
        P(),
        P(),
    )
    return jax.shard_map(
        shards,
        mesh=mesh,
        in_specs=placed,
        out_specs=(P(None, "slab", None), P("harm", None, None, "slab", None)),
        check_vma=False,
    )
```

profile of v0, /device:TPU:0, one launch (start us, length us, event | category | flops | bytes accessed | tf_op | source)
XLA Modules:
  0.0 381.3 jit_solution(15888537852805860238)
XLA Ops:
  7.2 1.1 pad_maximum_fusion.4
  8.4 1.3 collective-permute-start.1
  9.7 3.0 collective-permute-start
  13.4 9.0 %psum.35 = f32[]{:T(128)} all-reduce(f32[]{:T(128)} %multiply_reduce_fusion.36), channel_id=1, replica_groups=mesh['harm'=8,'slab'=4] {'slab'}, use_global_device_ids=true, to_apply=%region_1.2 | all-reduce | flops 1 | bytes 8 | tf_op jit(solution)/shard_map/psum | solution.py:118
  31.7 1.0 fusion.6
  33.8 1.1 add_bitcast_fusion.2
  35.1 66.6 %all-reduce.9.cloned.1.call-done = f32[4,2,2048]{2,1,0:T(2,128)} async-done(((f32[4,2,2048]{2,1,0:T(2,128)}), f32[4,2,2048]{2,1,0:T(2,128)}) %all-reduce.9.cloned.1.call-update) | async-done | bytes 65552 | tf_op jit(solution)/shard_map/psum | solution.py:133
  102.4 1.3 add_bitcast_fusion.5
  103.8 1.3 collective-permute-start.3
  105.1 3.2 collective-permute-start.2
  108.4 0.9 collective-permute-done.2
  119.1 0.8 fusion.231
  119.9 1.0 fusion.4
  122.0 1.1 add_bitcast_fusion.1
  123.4 68.7 %all-reduce.11.cloned.1.call-done = f32[4,2,2048]{2,1,0:T(2,128)} async-done(((f32[4,2,2048]{2,1,0:T(2,128)}), f32[4,2,2048]{2,1,0:T(2,128)}) %all-reduce.11.cloned.1.call-update) | async-done | bytes 65552 | tf_op jit(solution)/shard_map/psum | solution.py:133
  192.8 1.3 add_bitcast_fusion.4
  194.2 1.3 collective-permute-start.5
  195.5 3.3 collective-permute-start.4
  198.8 0.9 collective-permute-done.4
  209.5 0.8 fusion.229
  210.3 1.0 fusion.2
  212.4 1.1 add_bitcast_fusion
  213.8 68.7 %all-reduce.13.cloned.1.call-done = f32[4,2,2048]{2,1,0:T(2,128)} async-done(((f32[4,2,2048]{2,1,0:T(2,128)}), f32[4,2,2048]{2,1,0:T(2,128)}) %all-reduce.13.cloned.1.call-update) | async-done | bytes 65552 | tf_op jit(solution)/shard_map/psum | solution.py:133
  283.2 1.3 add_bitcast_fusion.3
  284.6 1.3 collective-permute-start.7
  285.9 3.3 collective-permute-start.6
  289.3 0.8 collective-permute-done.6
  299.1 0.8 fusion.227
  299.9 1.0 fusion
  302.0 1.7 multiply_add_fusion
  304.0 68.0 %all-reduce.15.cloned.1.call-done = f32[4,2,2048]{2,1,0:T(2,128)} async-done(((f32[4,2,2048]{2,1,0:T(2,128)}), f32[4,2,2048]{2,1,0:T(2,128)}) %all-reduce.15.cloned.1.call-update) | async-done | bytes 65552 | tf_op jit(solution)/shard_map/psum | solution.py:133
  372.8 2.0 multiply_add_fusion.1
  (307 shorter events, 44.4 us)
Async XLA Ops:
  7.2 23.9 %copy-start = (f32[5,5]{1,0:T(8,128)S(1)}, f32[5,5]{1,0:T(8,128)}, u32[]{:S(2)}) copy-start(f32[5,5]{1,0:T(8,128)} %param.10) | copy-start | bytes 304
  7.2 94.5 %all-reduce.9.cloned.1.call-start = ((), (), s32[]{:S(2)}) async-start(), calls=%async_computation | async-start | bytes 131072 | tf_op jit(solution)/shard_map/psum | solution.py:133
  7.2 16.6 %copy-start.1 = (f32[1,2,5,2,2048]{4,3,2,1,0:T(2,128)S(1)}, f32[1,2,5,2,2048]{4,3,2,1,0:T(2,128)}, u32[]{:S(2)}) copy-start(f32[1,2,5,2,2048]{4,3,2,1,0:T(2,128)} %param.6) | copy-start | bytes 491524
  8.4 15.4 %collective-permute-start.1 = (f32[3,5,2,2048]{3,2,1,0:T(2,128)S(1)}, f32[3,5,2,2048]{3,2,1,0:T(2,128)S(1)}, u32[]{:S(2)}, u32[]{:S(2)}) collective-permute-start(f32[3,5,2,2048]{3,2,1,0:T(2,128)S(1)} %pad_maximum_fusion.4), channel_id=1, source_target_pairs={{1,0},{2,1},{3,2},{5,4},{6,5},{7,6},{9,8},{10,9},{11,10},{13,12},{... | collective-permute-start | bytes 737288 | tf_op jit(solution)/shard_map/ppermute | solution.py:28
  9.7 14.1 %collective-permute-start = (f32[3,5,2,2048]{3,2,1,0:T(2,128)S(1)}, f32[3,5,2,2048]{3,2,1,0:T(2,128)S(1)}, u32[]{:S(2)}, u32[]{:S(2)}) collective-permute-start(f32[3,5,2,2048]{3,2,1,0:T(2,128)S(1)} %pad_maximum_fusion.4), channel_id=1, source_target_pairs={{0,1},{1,2},{2,3},{4,5},{5,6},{6,7},{8,9},{9,10},{10,11},{12,13},{... | collective-permute-start | bytes 737288 | tf_op jit(solution)/shard_map/ppermute | solution.py:26
  31.0 161.0 %all-reduce.11.cloned.1.call-start = ((), (), s32[]{:S(2)}) async-start(), calls=%async_computation.1 | async-start | bytes 131072 | tf_op jit(solution)/shard_map/psum | solution.py:133
  34.9 66.8 %copy-start.25 = (f32[5,2,1920]{2,1,0:T(2,128)S(1)}, f32[5,2,1920]{2,1,0:T(2,128)}, u32[]{:S(2)}) copy-start(f32[5,2,1920]{2,1,0:T(2,128)} %get-tuple-element.112) | copy-start | bytes 230404
  34.9 66.8 %copy-start.26 = (f32[5,2,1920]{2,1,0:T(2,128)S(1)}, f32[5,2,1920]{2,1,0:T(2,128)}, u32[]{:S(2)}) copy-start(f32[5,2,1920]{2,1,0:T(2,128)} %get-tuple-element.113) | copy-start | bytes 230404
  103.8 4.5 %collective-permute-start.3 = (f32[3,5,2,2048]{3,2,1,0:T(2,128)S(1)}, f32[3,5,2,2048]{3,2,1,0:T(2,128)S(1)}, u32[]{:S(2)}, u32[]{:S(2)}) collective-permute-start(f32[3,5,2,2048]{3,2,1,0:T(2,128)S(1)} %pad_maximum_fusion.5), channel_id=1, source_target_pairs={{1,0},{2,1},{3,2},{5,4},{6,5},{7,6},{9,8},{10,9},{11,10},{13,12},{... | collective-permute-start | bytes 737288 | tf_op jit(solution)/shard_map/ppermute | solution.py:28
  105.1 4.2 %collective-permute-start.2 = (f32[3,5,2,2048]{3,2,1,0:T(2,128)S(1)}, f32[3,5,2,2048]{3,2,1,0:T(2,128)S(1)}, u32[]{:S(2)}, u32[]{:S(2)}) collective-permute-start(f32[3,5,2,2048]{3,2,1,0:T(2,128)S(1)} %pad_maximum_fusion.5), channel_id=1, source_target_pairs={{0,1},{1,2},{2,3},{4,5},{5,6},{6,7},{8,9},{9,10},{10,11},{12,13},{... | collective-permute-start | bytes 737288 | tf_op jit(solution)/shard_map/ppermute | solution.py:26
  118.7 163.8 %all-reduce.13.cloned.1.call-start = ((), (), s32[]{:S(2)}) async-start(), calls=%async_computation.2 | async-start | bytes 131072 | tf_op jit(solution)/shard_map/psum | solution.py:133
  123.2 68.9 %copy-start.3 = (f32[5,2,1984]{2,1,0:T(2,128)S(1)}, f32[5,2,1984]{2,1,0:T(2,128)}, u32[]{:S(2)}) copy-start(f32[5,2,1984]{2,1,0:T(2,128)} %get-tuple-element.108) | copy-start | bytes 238084
  123.2 68.9 %copy-start.4 = (f32[5,2,1984]{2,1,0:T(2,128)S(1)}, f32[5,2,1984]{2,1,0:T(2,128)}, u32[]{:S(2)}) copy-start(f32[5,2,1984]{2,1,0:T(2,128)} %get-tuple-element.109) | copy-start | bytes 238084
  123.2 68.9 %copy-start.15 = (f32[5,2,1984]{2,1,0:T(2,128)S(1)}, f32[5,2,1984]{2,1,0:T(2,128)}, u32[]{:S(2)}) copy-start(f32[5,2,1984]{2,1,0:T(2,128)} %get-tuple-element.176) | copy-start | bytes 238084
  123.2 68.9 %copy-start.16 = (f32[5,2,1984]{2,1,0:T(2,128)S(1)}, f32[5,2,1984]{2,1,0:T(2,128)}, u32[]{:S(2)}) copy-start(f32[5,2,1984]{2,1,0:T(2,128)} %get-tuple-element.177) | copy-start | bytes 238084
  123.2 68.9 %copy-start.21 = (f32[5,2,1920]{2,1,0:T(2,128)S(1)}, f32[5,2,1920]{2,1,0:T(2,128)}, u32[]{:S(2)}) copy-start(f32[5,2,1920]{2,1,0:T(2,128)} %get-tuple-element.104) | copy-start | bytes 230404
  123.2 68.9 %copy-start.22 = (f32[5,2,1920]{2,1,0:T(2,128)S(1)}, f32[5,2,1920]{2,1,0:T(2,128)}, u32[]{:S(2)}) copy-start(f32[5,2,1920]{2,1,0:T(2,128)} %get-tuple-element.105) | copy-start | bytes 230404
  194.2 4.6 %collective-permute-start.5 = (f32[3,5,2,2048]{3,2,1,0:T(2,128)S(1)}, f32[3,5,2,2048]{3,2,1,0:T(2,128)S(1)}, u32[]{:S(2)}, u32[]{:S(2)}) collective-permute-start(f32[3,5,2,2048]{3,2,1,0:T(2,128)S(1)} %pad_maximum_fusion.6), channel_id=1, source_target_pairs={{1,0},{2,1},{3,2},{5,4},{6,5},{7,6},{9,8},{10,9},{11,10},{13,12},{... | collective-permute-start | bytes 737288 | tf_op jit(solution)/shard_map/ppermute | solution.py:28
  195.5 4.2 %collective-permute-start.4 = (f32[3,5,2,2048]{3,2,1,0:T(2,128)S(1)}, f32[3,5,2,2048]{3,2,1,0:T(2,128)S(1)}, u32[]{:S(2)}, u32[]{:S(2)}) collective-permute-start(f32[3,5,2,2048]{3,2,1,0:T(2,128)S(1)} %pad_maximum_fusion.6), channel_id=1, source_target_pairs={{0,1},{1,2},{2,3},{4,5},{5,6},{6,7},{8,9},{9,10},{10,11},{12,13},{... | collective-permute-start | bytes 737288 | tf_op jit(solution)/shard_map/ppermute | solution.py:26
  209.1 163.0 %all-reduce.15.cloned.1.call-start = ((), (), s32[]{:S(2)}) async-start(), calls=%async_computation.3 | async-start | bytes 131072 | tf_op jit(solution)/shard_map/psum | solution.py:133
  213.6 68.9 %copy-start.5 = (f32[5,2,1984]{2,1,0:T(2,128)S(1)}, f32[5,2,1984]{2,1,0:T(2,128)}, u32[]{:S(2)}) copy-start(f32[5,2,1984]{2,1,0:T(2,128)} %get-tuple-element.100) | copy-start | bytes 238084
  213.6 68.9 %copy-start.6 = (f32[5,2,1984]{2,1,0:T(2,128)S(1)}, f32[5,2,1984]{2,1,0:T(2,128)}, u32[]{:S(2)}) copy-start(f32[5,2,1984]{2,1,0:T(2,128)} %get-tuple-element.101) | copy-start | bytes 238084
  213.6 68.9 %copy-start.17 = (f32[5,2,1984]{2,1,0:T(2,128)S(1)}, f32[5,2,1984]{2,1,0:T(2,128)}, u32[]{:S(2)}) copy-start(f32[5,2,1984]{2,1,0:T(2,128)} %get-tuple-element.172) | copy-start | bytes 238084
  213.6 68.9 %copy-start.18 = (f32[5,2,1984]{2,1,0:T(2,128)S(1)}, f32[5,2,1984]{2,1,0:T(2,128)}, u32[]{:S(2)}) copy-start(f32[5,2,1984]{2,1,0:T(2,128)} %get-tuple-element.173) | copy-start | bytes 238084
  213.6 68.9 %copy-start.23 = (f32[5,2,1920]{2,1,0:T(2,128)S(1)}, f32[5,2,1920]{2,1,0:T(2,128)}, u32[]{:S(2)}) copy-start(f32[5,2,1920]{2,1,0:T(2,128)} %get-tuple-element.96) | copy-start | bytes 230404
  213.6 68.9 %copy-start.24 = (f32[5,2,1920]{2,1,0:T(2,128)S(1)}, f32[5,2,1920]{2,1,0:T(2,128)}, u32[]{:S(2)}) copy-start(f32[5,2,1920]{2,1,0:T(2,128)} %get-tuple-element.97) | copy-start | bytes 230404
  284.6 4.6 %collective-permute-start.7 = (f32[3,5,2,2048]{3,2,1,0:T(2,128)S(1)}, f32[3,5,2,2048]{3,2,1,0:T(2,128)S(1)}, u32[]{:S(2)}, u32[]{:S(2)}) collective-permute-start(f32[3,5,2,2048]{3,2,1,0:T(2,128)S(1)} %pad_maximum_fusion.7), channel_id=1, source_target_pairs={{1,0},{2,1},{3,2},{5,4},{6,5},{7,6},{9,8},{10,9},{11,10},{13,12},{... | collective-permute-start | bytes 737288 | tf_op jit(solution)/shard_map/ppermute | solution.py:28
  285.9 4.2 %collective-permute-start.6 = (f32[3,5,2,2048]{3,2,1,0:T(2,128)S(1)}, f32[3,5,2,2048]{3,2,1,0:T(2,128)S(1)}, u32[]{:S(2)}, u32[]{:S(2)}) collective-permute-start(f32[3,5,2,2048]{3,2,1,0:T(2,128)S(1)} %pad_maximum_fusion.7), channel_id=1, source_target_pairs={{0,1},{1,2},{2,3},{4,5},{5,6},{6,7},{8,9},{9,10},{10,11},{12,13},{... | collective-permute-start | bytes 737288 | tf_op jit(solution)/shard_map/ppermute | solution.py:26
  303.9 68.2 %copy-start.13 = (f32[5,2,1984]{2,1,0:T(2,128)S(1)}, f32[5,2,1984]{2,1,0:T(2,128)}, u32[]{:S(2)}) copy-start(f32[5,2,1984]{2,1,0:T(2,128)} %get-tuple-element.168) | copy-start | bytes 238084
  303.9 68.2 %copy-start.14 = (f32[5,2,1984]{2,1,0:T(2,128)S(1)}, f32[5,2,1984]{2,1,0:T(2,128)}, u32[]{:S(2)}) copy-start(f32[5,2,1984]{2,1,0:T(2,128)} %get-tuple-element.169) | copy-start | bytes 238084
  303.9 68.2 %copy-start.19 = (f32[5,2,1920]{2,1,0:T(2,128)S(1)}, f32[5,2,1920]{2,1,0:T(2,128)}, u32[]{:S(2)}) copy-start(f32[5,2,1920]{2,1,0:T(2,128)} %get-tuple-element.88) | copy-start | bytes 230404
  303.9 68.2 %copy-start.20 = (f32[5,2,1920]{2,1,0:T(2,128)S(1)}, f32[5,2,1920]{2,1,0:T(2,128)}, u32[]{:S(2)}) copy-start(f32[5,2,1920]{2,1,0:T(2,128)} %get-tuple-element.89) | copy-start | bytes 230404
  (37 other events, 37.7 us)
Sparse Core Ops, SparseCore 0:
  31.2 70.4 all-reduce.8
  118.8 73.2 all-reduce.10
  209.2 73.2 all-reduce.12
  298.9 73.1 all-reduce.14
where the time goes:
time: 382 us; the launch traced here: 381 us
  waiting for transfers between devices  275 us (72%)
  local copies, waits for them, and re-layouts  29.8 us (8%)
  other arithmetic  23.4 us (6%)
  starting transfers between devices  18.2 us (5%)
  between operations  16.7 us (4%)
  matrix products  9.5 us (2%)
  blocking collectives  9.02 us (2%)
    psum x4, waiting for transfers between devices, shards(): forcing_terms = lax.psum(partial_terms, 'harm')  272 us
    ppermute x4, starting transfers between devices, with_halo(): lax.ppermute(tail, axis, [(i, (i + 1) % count) for i in range(ends)])  12.8 us
    dot_general x16, matrix products, apply_matrix(): jnp.einsum('ab,...bxp->...axp', matrix, values, precision=lax.Precision.H...  9.5 us
    psum x1, blocking collectives, shards(): speed_total = lax.psum(jnp.sum(mean_flow[1] * mean_flow[1]), 'slab')  9.02 us
    slice x16, local copies, waits for them, and re-layouts, fourth_across(): jnp.roll(values, -NZ, axis=-1)  8.58 us
  transfers between devices with their start and end apart: 12, of which 7 were waited for; matrix products, arithmetic and copies ran while one was open for 4% of the time, Pallas kernels for 0%

commit v1 on v0

--- a/solution.py
+++ b/solution.py
@@ -1,6 +1,10 @@
+import functools
+
 import jax
 import jax.numpy as jnp
 from jax import lax
+from jax.experimental import pallas as pl
+from jax.experimental.pallas import tpu as pltpu
 from jax.sharding import PartitionSpec as P
 
 NZ = 64
@@ -137,6 +141,399 @@
     return (mean_now, harm_now)
 
 
+MESH_ID = pl.DeviceIdType.MESH
+LANES = 128
+ROWS = 8
+F32 = jnp.float32
+
+
+def swap_bit(pair, stride, bit):
+    low, high = pair
+    return (
+        jnp.where(bit == 0, low, pltpu.roll(high, stride, 1)),
+        jnp.where(bit == 0, pltpu.roll(low, LANES - stride, 1), high),
+    )
+
+
+def radial_kernel(
+    dims, h_ref, m_ref, f_ref, w_ref, jx_ref, jy_ref, mo_ref, ho_ref,
+    rows, send, recv, mrecv, state, first, omega, mean, mean0, back, home,
+    hs_sem, hr_sem, ms_sem, mr_sem, bs_sem, br_sem,
+):
+    nh, ns, nvar, cells, tiles = dims
+    nd = nh * ns
+    mh, ms = lax.axis_index("harm"), lax.axis_index("slab")
+    me = mh * ns + ms
+    nx = ns * cells
+
+    barrier = pltpu.get_barrier_semaphore()
+
+    def greet(o, _):
+        d = lax.rem(me + o, nd)
+        pl.semaphore_signal(
+            barrier, inc=1, device_id=(d // ns, lax.rem(d, ns)), device_id_type=MESH_ID
+        )
+        return 0
+
+    lax.fori_loop(1, nd, greet, 0)
+
+    lane_all = lax.broadcasted_iota(jnp.int32, (nd, LANES), 1)
+    low_bit = lane_all & 1
+    high_bit = (lane_all >> 2) & 1
+
+    def place(at, value):
+        rows[pl.ds(cells * at, cells), :] = value
+
+    for a in range(nvar):
+        for c in range(2):
+            place(2 * a + c, h_ref[0, c, a])
+    place(2 * nvar, m_ref[nvar - 1])
+    place(2 * nvar + 1, w_ref[...].astype(F32))
+    for a in range(nvar - 1):
+        place(2 * nvar + 2 + a, m_ref[a])
+
+    def block_of(g):
+        return g if g < nvar else g + 1
+
+    for grp in range(4):
+        mat = jnp.concatenate(
+            [rows[ROWS * grp : ROWS * grp + ROWS, LANES * t : LANES * t + LANES] for t in range(tiles)],
+            axis=0,
+        )
+        turned = mat.T
+        part = [[turned[nd * (2 * i + j) : nd * (2 * i + j) + nd] for j in range(2)] for i in range(2)]
+        cols = [swap_bit((part[0][j], part[1][j]), 4, high_bit) for j in range(2)]
+        for g1 in range(2):
+            outs = swap_bit((cols[0][g1], cols[1][g1]), 1, low_bit)
+            for g0 in range(2):
+                send[:, block_of(2 * grp + g1), g0, :] = outs[g0]
+    speed = m_ref[1]
+    partial_sum = jnp.sum(jnp.sum(speed * speed, axis=1, keepdims=True), axis=0, keepdims=True)
+    rate_own = jnp.full((1, 1), 0.25 * f_ref[0].astype(F32), F32)
+    send[:, nvar, 0, :] = jnp.broadcast_to(rate_own, (nd, LANES))
+    send[:, nvar, 1, :] = jnp.broadcast_to(partial_sum, (nd, LANES))
+
+    recv[mh, ms] = send[me, 0 : nvar + 1]
+    mrecv[ms] = send[me, nvar + 1 : nvar + 4]
+
+    pl.semaphore_wait(barrier, nd - 1)
+
+    def out_copy(d):
+        return pltpu.make_async_remote_copy(
+            src_ref=send.at[d, pl.ds(0, nvar + 1)],
+            dst_ref=recv.at[mh, ms],
+            send_sem=hs_sem.at[d],
+            recv_sem=hr_sem.at[me],
+            device_id=(d // ns, lax.rem(d, ns)),
+            device_id_type=MESH_ID,
+        )
+
+    def in_copy(d):
+        return pltpu.make_async_remote_copy(
+            src_ref=send.at[d, pl.ds(0, nvar + 1)],
+            dst_ref=recv.at[d // ns, lax.rem(d, ns)],
+            send_sem=hs_sem.at[d],
+            recv_sem=hr_sem.at[d],
+            device_id=(d // ns, lax.rem(d, ns)),
+            device_id_type=MESH_ID,
+        )
+
+    def mean_out(s):
+        return pltpu.make_async_remote_copy(
+            src_ref=send.at[mh * ns + s, pl.ds(nvar + 1, 3)],
+            dst_ref=mrecv.at[ms],
+            send_sem=ms_sem.at[s],
+            recv_sem=mr_sem.at[ms],
+            device_id=(mh, s),
+            device_id_type=MESH_ID,
+        )
+
+    def mean_in(s):
+        return pltpu.make_async_remote_copy(
+            src_ref=send.at[mh * ns + s, pl.ds(nvar + 1, 3)],
+            dst_ref=mrecv.at[s],
+            send_sem=ms_sem.at[s],
+            recv_sem=mr_sem.at[s],
+            device_id=(mh, s),
+            device_id_type=MESH_ID,
+        )
+
+    def go(o, _):
+        out_copy(lax.rem(me + o, nd)).start()
+        return 0
+
+    def go_mean(o, _):
+        mean_out(lax.rem(ms + o, ns)).start()
+        return 0
+
+    def land(o, _):
+        in_copy(lax.rem(me + o, nd)).wait_recv()
+        return 0
+
+    def land_mean(o, _):
+        mean_in(lax.rem(ms + o, ns)).wait_recv()
+        return 0
+
+    lax.fori_loop(1, nd, go, 0)
+    lax.fori_loop(1, ns, go_mean, 0)
+    lax.fori_loop(1, nd, land, 0)
+    lax.fori_loop(1, ns, land_mean, 0)
+
+    lane = lax.broadcasted_iota(jnp.int32, (nx, LANES), 1)
+    cell = lax.broadcasted_iota(jnp.int32, (nx, LANES), 0)
+    second = (lane >> 1) & 1
+    is_real = second == 0
+
+    def other(value):
+        return jnp.where(is_real, pltpu.roll(value, LANES - 2, 1), pltpu.roll(value, 2, 1))
+
+    def spread(value):
+        turned = other(value)
+        return jnp.where(is_real, value, turned), jnp.where(is_real, turned, value)
+
+    def assemble(k, _):
+        for s in range(ns):
+            for a in range(nvar):
+                got = recv[k, s, a]
+                state[k, a, cells * s : cells * s + cells, :] = got
+                first[k, a, cells * s : cells * s + cells, :] = got
+        omega[k] = jnp.broadcast_to(recv[k, 0, nvar, 0:1, :], (nx, LANES))
+        return 0
+
+    lax.fori_loop(0, nh, assemble, 0)
+    packed = []
+    for b in range(3):
+        for s in range(ns):
+            mean[b, cells * s : cells * s + cells, :] = mrecv[s, b]
+        packed.append(mean[b])
+    m4, wall = spread(packed[0])
+    m0, m1 = spread(packed[1])
+    m2, m3 = spread(packed[2])
+    for a, value in enumerate((m0, m1, m2, m3, m4)):
+        mean[a] = value
+        mean0[a] = value
+    total = recv[0, 0, nvar, 1:2, :]
+    for s in range(1, ns):
+        total = total + recv[0, s, nvar, 1:2, :]
+    count = nx * tiles * LANES
+    time_step = jnp.broadcast_to(0.9 / (1.0 + jnp.sqrt(total / count)), (nx, LANES))
+    wall2 = 2.0 * wall
+    z = (lane & 1) * nd + me
+    radius = 0.5 + (z.astype(F32) + 0.5) / (2 * nd)
+    inv_r = 1.0 / radius
+
+    mp1 = jnp.where(cell < nx - 1, 1.0, 0.0).astype(F32)
+    mm1 = jnp.where(cell > 0, 1.0, 0.0).astype(F32)
+    mp2 = jnp.where(cell < nx - 2, 1.0, 0.0).astype(F32)
+    mm2 = jnp.where(cell > 1, 1.0, 0.0).astype(F32)
+
+    def xp(v, n):
+        return pltpu.roll(v, nx - n, 0)
+
+    def xm(v, n):
+        return pltpu.roll(v, n, 0)
+
+    def yp(v, n):
+        return pltpu.roll(v, LANES - 4 * n, 1)
+
+    def ym(v, n):
+        return pltpu.roll(v, 4 * n, 1)
+
+    def pieces(v, fwd, bwd):
+        xp1, xm1 = xp(v, 1), xm(v, 1)
+        yp1, ym1 = yp(v, 1), ym(v, 1)
+        fourth = (
+            mp2 * xp(v, 2) + mm2 * xm(v, 2) + 12.0 * v + yp(v, 2) + ym(v, 2)
+            - 4.0 * (mp1 * xp1 + mm1 * xm1 + yp1 + ym1)
+        )
+        return fwd * xp1 - bwd * xm1, yp1 - ym1, fourth
+
+    def mix(us, vs, a):
+        flux = jx_ref[a, 0] * us[0]
+        for b in range(1, nvar):
+            flux = flux + jx_ref[a, b] * us[b]
+        for b in range(nvar):
+            flux = flux + jy_ref[a, b] * vs[b]
+        return 0.5 * flux
+
+    pairs = ((1, 1), (1, 2), (1, 3), (2, 2), (2, 3), (3, 3), (4, 1), (4, 2), (4, 3))
+
+    def section(i, _):
+        rate = jnp.where(i == 0, 0.25, jnp.where(i == 1, 1.0 / 3.0, jnp.where(i == 2, 0.5, 1.0))).astype(F32)
+        step = rate * time_step
+        mc = mean[1]
+        fwd = mp1 * xp(mc, 1)
+        bwd = mm1 * xm(mc, 1)
+
+        def one(k, acc):
+            hs = [state[k, a] for a in range(nvar)]
+            acc = tuple(s + hs[p] * hs[q] for s, (p, q) in zip(acc, pairs))
+            om = jnp.where(is_real, omega[k], -omega[k])
+            got = [pieces(h, fwd, bwd) for h in hs]
+            us, vs = [g[0] for g in got], [g[1] for g in got]
+            for a in range(nvar):
+                res = om * other(hs[a]) - mix(us, vs, a) - 0.05 * got[a][2] - wall2 * hs[a]
+                state[k, a] = first[k, a] + step * res
+            return acc
+
+        zero = jnp.zeros((nx, LANES), F32)
+        acc = lax.fori_loop(0, nh, one, (zero,) * len(pairs))
+        s = [0.5 * (v + other(v)) for v in acc]
+
+        def gx(v):
+            return 0.5 * (mp1 * xp(v, 1) - mm1 * xm(v, 1))
+
+        def gy(v):
+            return 0.5 * (yp(v, 1) - ym(v, 1))
+
+        force = (
+            zero,
+            -gx(s[0]) - gy(s[1]),
+            -gx(s[1]) - gy(s[3]) - 2.0 * s[4] * inv_r,
+            -gx(s[2]) - gy(s[4]) + (s[3] - s[5]) * inv_r,
+            -gx(s[6]) - gy(s[7]) - s[8] * inv_r,
+        )
+        means = [mean[a] for a in range(nvar)]
+        got = [pieces(m, mp1, mm1) for m in means]
+        us, vs = [g[0] for g in got], [g[1] for g in got]
+        for a in range(nvar):
+            res = force[a] - mix(us, vs, a) - 0.05 * got[a][2]
+            mean[a] = mean0[a] + step * res
+        return 0
+
+    lax.fori_loop(0, 4, section, 0)
+
+    def join(even, odd):
+        return jnp.where(is_real, even, odd)
+
+    packs = (mean[4], join(mean[0], mean[1]), join(mean[2], mean[3]))
+
+    def leave(k, _):
+        for s in range(ns):
+            for a in range(nvar):
+                back[k, s, a] = state[k, a, cells * s : cells * s + cells, :]
+            for b in range(3):
+                back[k, s, nvar + b] = packs[b][cells * s : cells * s + cells, :]
+        return 0
+
+    lax.fori_loop(0, nh, leave, 0)
+    home[me] = back[mh, ms]
+
+    def back_copy(d, slot):
+        return pltpu.make_async_remote_copy(
+            src_ref=back.at[d // ns, lax.rem(d, ns)],
+            dst_ref=home.at[slot],
+            send_sem=bs_sem.at[d],
+            recv_sem=br_sem.at[slot],
+            device_id=(d // ns, lax.rem(d, ns)),
+            device_id_type=MESH_ID,
+        )
+
+    def go_back(o, _):
+        d = lax.rem(me + o, nd)
+        back_copy(d, me).start()
+        return 0
+
+    def land_back(o, _):
+        d = lax.rem(me + o, nd)
+        back_copy(d, d).wait_recv()
+        return 0
+
+    lax.fori_loop(1, nd, go_back, 0)
+    lax.fori_loop(1, nd, land_back, 0)
+
+    for grp in range(4):
+        cols = []
+        for g1 in range(2):
+            cols.append(swap_bit([home[:, 2 * grp + g1, g0, :] for g0 in range(2)], 1, low_bit))
+        part = [swap_bit((cols[0][j], cols[1][j]), 4, high_bit) for j in range(2)]
+        mat = jnp.concatenate([part[j][i] for i in range(2) for j in range(2)], axis=0)
+        turned = mat.T
+        for t in range(tiles):
+            rows[ROWS * grp : ROWS * grp + ROWS, LANES * t : LANES * t + LANES] = turned[
+                ROWS * t : ROWS * t + ROWS
+            ]
+
+    def take(at):
+        return rows[pl.ds(cells * at, cells), :]
+
+    for a in range(nvar):
+        for c in range(2):
+            ho_ref[0, c, a] = take(2 * a + c)
+    mo_ref[nvar - 1] = take(2 * nvar)
+    for a in range(nvar - 1):
+        mo_ref[a] = take(2 * nvar + 2 + a)
+
+    def sent(o, _):
+        d = lax.rem(me + o, nd)
+        out_copy(d).wait_send()
+        back_copy(d, me).wait_send()
+        return 0
+
+    def sent_mean(o, _):
+        mean_out(lax.rem(ms + o, ns)).wait_send()
+        return 0
+
+    lax.fori_loop(1, nd, sent, 0)
+    lax.fori_loop(1, ns, sent_mean, 0)
+
+
+def radial_shards(nh, ns, harmonics, mean_flow, freq_index, wall_mask, jacobian_x, jacobian_y):
+    nvar, cells, planes = mean_flow.shape
+    nd, nx = nh * ns, ns * cells
+    vmem = pl.BlockSpec(memory_space=pltpu.VMEM)
+    smem = pl.BlockSpec(memory_space=pltpu.SMEM)
+    dims = (nh, ns, nvar, cells, planes // LANES)
+    field = (nx, LANES)
+    piece = (cells, LANES)
+    return pl.pallas_call(
+        functools.partial(radial_kernel, dims),
+        out_shape=(
+            jax.ShapeDtypeStruct(mean_flow.shape, F32),
+            jax.ShapeDtypeStruct(harmonics.shape, F32),
+        ),
+        in_specs=[vmem, vmem, smem, vmem, smem, smem],
+        out_specs=(vmem, vmem),
+        scratch_shapes=[
+            pltpu.VMEM((4 * ROWS, planes), F32),
+            pltpu.VMEM((nd, nvar + 4, *piece), F32),
+            pltpu.VMEM((nh, ns, nvar + 1, *piece), F32),
+            pltpu.VMEM((ns, 3, *piece), F32),
+            pltpu.VMEM((nh, nvar, *field), F32),
+            pltpu.VMEM((nh, nvar, *field), F32),
+            pltpu.VMEM((nh, *field), F32),
+            pltpu.VMEM((nvar, *field), F32),
+            pltpu.VMEM((nvar, *field), F32),
+            pltpu.VMEM((nh, ns, nvar + 3, *piece), F32),
+            pltpu.VMEM((nd, nvar + 3, *piece), F32),
+            pltpu.SemaphoreType.DMA((nd,)),
+            pltpu.SemaphoreType.DMA((nd,)),
+            pltpu.SemaphoreType.DMA((ns,)),
+            pltpu.SemaphoreType.DMA((ns,)),
+            pltpu.SemaphoreType.DMA((nd,)),
+            pltpu.SemaphoreType.DMA((nd,)),
+        ],
+        compiler_params=pltpu.CompilerParams(collective_id=0, has_side_effects=True),
+    )(harmonics, mean_flow, freq_index, wall_mask, jacobian_x, jacobian_y)
+
+
+def fits_radial(nh, ns, harmonics, mean_flow):
+    owned, parts, nvar, cells, planes = harmonics.shape
+    return (
+        NZ == 2 * nh * ns
+        and LANES == 2 * NZ
+        and (owned, parts, nvar, cells) == (1, 2, 5, 2)
+        and ns * cells == ROWS
+        and planes == 16 * LANES
+    )
+
+
+def either(nh, ns, harmonics, mean_flow, *rest):
+    if fits_radial(nh, ns, harmonics, mean_flow):
+        return radial_shards(nh, ns, harmonics, mean_flow, *rest)
+    return shards(harmonics, mean_flow, *rest)
+
+
 def solution(mesh):
     placed = (
         P("harm", None, None, "slab", None),
@@ -147,7 +544,7 @@
         P(),
     )
     return jax.shard_map(
-        shards,
+        functools.partial(either, mesh.shape["harm"], mesh.shape["slab"]),
         mesh=mesh,
         in_specs=placed,
         out_specs=(P(None, "slab", None), P("harm", None, None, "slab", None)),

time: 382 us -> 31.2 us (0.08)
  waiting for transfers between devices: 275 us -> 0 us
  local copies, waits for them, and re-layouts: 29.8 us -> 2.24 us
  Pallas kernels: 0 us -> 27.2 us
  other arithmetic: 23.4 us -> 0 us
  starting transfers between devices: 18.2 us -> 0 us
  between operations: 16.7 us -> 1.29 us
  matrix products: 9.5 us -> 0 us
  blocking collectives: 9.02 us -> 0 us
    psum x4 -> x0, waiting for transfers between devices: 272 us -> none  [shards(): forcing_terms = lax.psum(partial_terms, 'harm')]
    pallas_call x0 -> x1, Pallas kernels: none -> 27.2 us  [radial_shards(): pl.pallas_call(functools.partial(radial_kernel, dims), out_shape=(jax.Sha...]
    slice x56 -> x0, local copies, waits for them, and re-layouts: 20.5 us -> none  [the longest x16 8.58 us: fourth_across(): jnp.roll(values, -NZ, axis=-1)]
    ppermute x8 -> x0, starting transfers between devices: 18 us -> none  [the longest x4 12.8 us: with_halo(): lax.ppermute(tail, axis, [(i, (i + 1) % count) for i in range(ends)])]
    dot_general x16 -> x0, matrix products: 9.5 us -> none  [apply_matrix(): jnp.einsum('ab,...bxp->...axp', matrix, values, precision=lax.Precision.H...]
    psum x1 -> x0, blocking collectives: 9.02 us -> none  [shards(): speed_total = lax.psum(jnp.sum(mean_flow[1] * mean_flow[1]), 'slab')]
    unnamed x114 -> x4, local copies, waits for them, and re-layouts: 6.36 us -> 2.24 us
    broadcast_in_dim x3 -> x0, other arithmetic: 4.01 us -> none  [shards(): mean_now[None]]
  transfers between devices with their start and end apart: 12 -> 0, of which waited for: 7 -> 0; matrix products, arithmetic and copies ran while one was open for 4% -> 0% of each run, Pallas kernels for 0% -> 0%
where the time goes in v1:
time: 31.2 us; the launch traced here: 30.7 us
  Pallas kernels  27.2 us (87%)
  local copies, waits for them, and re-layouts  2.24 us (7%)
  between operations  1.29 us (4%)
    pallas_call x1, Pallas kernels, radial_shards(): pl.pallas_call(functools.partial(radial_kernel, dims), out_shape=(jax.Sha...  27.2 us
    unnamed x4, local copies, waits for them, and re-layouts  2.24 us

profile of v1, /device:TPU:0, one launch (start us, length us, event | category | flops | bytes accessed | tf_op | source)
XLA Modules:
  0.0 30.7 jit_solution(18153705289648024624)
XLA Ops:
  1.3 27.2 %shard_map.77 = (f32[5,2,2048]{2,1,0:T(2,128)}, f32[1,2,5,2,2048]{4,3,2,1,0:T(2,128)}) custom-call(f32[1,2,5,2,2048]{4,3,2,1,0:T(2,128)} %h_ref.1, f32[5,2,2048]{2,1,0:T(2,128)} %m_ref.1, s32[1]{0:T(128)S(6)} %copy.10.f_ref, s32[2,2048]{1,0:T(2,128)} %w_ref.1, f32[5,5]{1,0:T(8,128)} %jx_ref.1, f32[5,5]{1,0:T(8,128)} %jy_ref.1), custom_call_target="tpu_custom_call" | custom-call | tf_op jit(solution)/shard_map/pallas_call | solution.py:489
  28.5 0.0 copy-start
  28.5 1.6 %copy.11 = f32[5,2,2048]{2,1,0:T(2,128)} copy(f32[5,2,2048]{2,1,0:T(2,128)} %get-tuple-element.4) | data formatting | bytes 163840
  30.1 0.0 copy-done
  30.1 0.7 %copy.12 = f32[1,2,5,2,2048]{4,3,2,1,0:T(2,128)} copy(f32[1,2,5,2,2048]{4,3,2,1,0:T(2,128)S(1)} %copy-done) | data formatting | bytes 327680
Async XLA Ops:
  28.5 1.6 %copy-start = (f32[1,2,5,2,2048]{4,3,2,1,0:T(2,128)S(1)}, f32[1,2,5,2,2048]{4,3,2,1,0:T(2,128)}, u32[]{:S(2)}) copy-start(f32[1,2,5,2,2048]{4,3,2,1,0:T(2,128)} %get-tuple-element.5) | copy-start | bytes 491524

commit v2 on v1

--- a/solution.py
+++ b/solution.py
@@ -156,8 +156,8 @@
 
 
 def radial_kernel(
-    dims, h_ref, m_ref, f_ref, w_ref, jx_ref, jy_ref, mo_ref, ho_ref,
-    rows, send, recv, mrecv, state, first, omega, mean, mean0, back, home,
+    dims, h_any, m_any, f_ref, w_any, jx_ref, jy_ref, mo_ref, ho_ref,
+    h_ref, m_ref, w_ref, in_sem, rows, send, recv, mrecv, state, first, omega, mean, mean0, back, home,
     hs_sem, hr_sem, ms_sem, mr_sem, bs_sem, br_sem,
 ):
     nh, ns, nvar, cells, tiles = dims
@@ -168,14 +168,42 @@
 
     barrier = pltpu.get_barrier_semaphore()
 
-    def greet(o, _):
-        d = lax.rem(me + o, nd)
+    def flip(index, bits):
+        out = index
+        weight = 1
+        while weight <= bits:
+            if bits & weight:
+                out = out + weight * (1 - 2 * lax.rem(index // weight, 2))
+            weight *= 2
+        return out
+
+    def flip_by(index, bits):
+        out = index
+        weight = 1
+        while weight < nh:
+            out = out + lax.rem(bits // weight, 2) * weight * (1 - 2 * lax.rem(index // weight, 2))
+            weight *= 2
+        return out
+
+    def reach(offset):
+        oh, os = offset
+        return min(oh >> 1, 2) + (oh & 1) + (os >> 1) + 0.3 * (os & 1)
+
+    far_first = sorted(
+        [(oh, os) for oh in range(nh) for os in range(ns) if oh or os], key=reach, reverse=True
+    )
+    for oh, os in far_first:
         pl.semaphore_signal(
-            barrier, inc=1, device_id=(d // ns, lax.rem(d, ns)), device_id_type=MESH_ID
-        )
-        return 0
-
-    lax.fori_loop(1, nd, greet, 0)
+            barrier, inc=1, device_id=(flip(mh, oh), flip(ms, os)), device_id_type=MESH_ID
+        )
+    loads = [
+        pltpu.make_async_copy(src, dst, in_sem.at[i])
+        for i, (src, dst) in enumerate(((h_any, h_ref), (m_any, m_ref), (w_any, w_ref)))
+    ]
+    for load in loads:
+        load.start()
+    for load in loads:
+        load.wait()
 
     lane_all = lax.broadcasted_iota(jnp.int32, (nd, LANES), 1)
     low_bit = lane_all & 1
@@ -218,66 +246,43 @@
 
     pl.semaphore_wait(barrier, nd - 1)
 
-    def out_copy(d):
+    def out_copy(kd, sd):
+        d = kd * ns + sd
         return pltpu.make_async_remote_copy(
             src_ref=send.at[d, pl.ds(0, nvar + 1)],
             dst_ref=recv.at[mh, ms],
             send_sem=hs_sem.at[d],
             recv_sem=hr_sem.at[me],
-            device_id=(d // ns, lax.rem(d, ns)),
+            device_id=(kd, sd),
             device_id_type=MESH_ID,
         )
 
-    def in_copy(d):
+    def in_copy(kd, sd):
+        d = kd * ns + sd
         return pltpu.make_async_remote_copy(
             src_ref=send.at[d, pl.ds(0, nvar + 1)],
-            dst_ref=recv.at[d // ns, lax.rem(d, ns)],
+            dst_ref=recv.at[kd, sd],
             send_sem=hs_sem.at[d],
             recv_sem=hr_sem.at[d],
-            device_id=(d // ns, lax.rem(d, ns)),
+            device_id=(kd, sd),
             device_id_type=MESH_ID,
         )
 
-    def mean_out(s):
+    def mean_copy(s, slot):
         return pltpu.make_async_remote_copy(
             src_ref=send.at[mh * ns + s, pl.ds(nvar + 1, 3)],
-            dst_ref=mrecv.at[ms],
+            dst_ref=mrecv.at[slot],
             send_sem=ms_sem.at[s],
-            recv_sem=mr_sem.at[ms],
+            recv_sem=mr_sem.at[slot],
             device_id=(mh, s),
             device_id_type=MESH_ID,
         )
 
-    def mean_in(s):
-        return pltpu.make_async_remote_copy(
-            src_ref=send.at[mh * ns + s, pl.ds(nvar + 1, 3)],
-            dst_ref=mrecv.at[s],
-            send_sem=ms_sem.at[s],
-            recv_sem=mr_sem.at[s],
-            device_id=(mh, s),
-            device_id_type=MESH_ID,
-        )
-
-    def go(o, _):
-        out_copy(lax.rem(me + o, nd)).start()
-        return 0
-
-    def go_mean(o, _):
-        mean_out(lax.rem(ms + o, ns)).start()
-        return 0
-
-    def land(o, _):
-        in_copy(lax.rem(me + o, nd)).wait_recv()
-        return 0
-
-    def land_mean(o, _):
-        mean_in(lax.rem(ms + o, ns)).wait_recv()
-        return 0
-
-    lax.fori_loop(1, nd, go, 0)
-    lax.fori_loop(1, ns, go_mean, 0)
-    lax.fori_loop(1, nd, land, 0)
-    lax.fori_loop(1, ns, land_mean, 0)
+    for oh, os in far_first:
+        out_copy(flip(mh, oh), flip(ms, os)).start()
+        if oh == 1 and os == ns - 1:
+            for o in range(ns - 1, 0, -1):
+                mean_copy(flip(ms, o), ms).start()
 
     lane = lax.broadcasted_iota(jnp.int32, (nx, LANES), 1)
     cell = lax.broadcasted_iota(jnp.int32, (nx, LANES), 0)
@@ -291,16 +296,10 @@
         turned = other(value)
         return jnp.where(is_real, value, turned), jnp.where(is_real, turned, value)
 
-    def assemble(k, _):
-        for s in range(ns):
-            for a in range(nvar):
-                got = recv[k, s, a]
-                state[k, a, cells * s : cells * s + cells, :] = got
-                first[k, a, cells * s : cells * s + cells, :] = got
-        omega[k] = jnp.broadcast_to(recv[k, 0, nvar, 0:1, :], (nx, LANES))
-        return 0
-
-    lax.fori_loop(0, nh, assemble, 0)
+    for o in range(1, ns):
+        peer = flip(ms, o)
+        in_copy(mh, peer).wait_recv()
+        mean_copy(peer, peer).wait_recv()
     packed = []
     for b in range(3):
         for s in range(ns):
@@ -312,9 +311,9 @@
     for a, value in enumerate((m0, m1, m2, m3, m4)):
         mean[a] = value
         mean0[a] = value
-    total = recv[0, 0, nvar, 1:2, :]
+    total = recv[mh, 0, nvar, 1:2, :]
     for s in range(1, ns):
-        total = total + recv[0, s, nvar, 1:2, :]
+        total = total + recv[mh, s, nvar, 1:2, :]
     count = nx * tiles * LANES
     time_step = jnp.broadcast_to(0.9 / (1.0 + jnp.sqrt(total / count)), (nx, LANES))
     wall2 = 2.0 * wall
@@ -358,34 +357,33 @@
 
     pairs = ((1, 1), (1, 2), (1, 3), (2, 2), (2, 3), (3, 3), (4, 1), (4, 2), (4, 3))
 
-    def section(i, _):
-        rate = jnp.where(i == 0, 0.25, jnp.where(i == 1, 1.0 / 3.0, jnp.where(i == 2, 0.5, 1.0))).astype(F32)
-        step = rate * time_step
-        mc = mean[1]
-        fwd = mp1 * xp(mc, 1)
-        bwd = mm1 * xm(mc, 1)
-
-        def one(k, acc):
-            hs = [state[k, a] for a in range(nvar)]
-            acc = tuple(s + hs[p] * hs[q] for s, (p, q) in zip(acc, pairs))
-            om = jnp.where(is_real, omega[k], -omega[k])
-            got = [pieces(h, fwd, bwd) for h in hs]
-            us, vs = [g[0] for g in got], [g[1] for g in got]
-            for a in range(nvar):
-                res = om * other(hs[a]) - mix(us, vs, a) - 0.05 * got[a][2] - wall2 * hs[a]
-                state[k, a] = first[k, a] + step * res
-            return acc
-
-        zero = jnp.zeros((nx, LANES), F32)
-        acc = lax.fori_loop(0, nh, one, (zero,) * len(pairs))
+    zero = jnp.zeros((nx, LANES), F32)
+    empty = (zero,) * len(pairs)
+
+    def products(acc, hs):
+        return tuple(s + hs[p] * hs[q] for s, (p, q) in zip(acc, pairs))
+
+    def advance(k, hs, om, edges, step):
+        om = jnp.where(is_real, om, -om)
+        got = [pieces(h, *edges) for h in hs]
+        us, vs = [g[0] for g in got], [g[1] for g in got]
+        news = []
+        for a in range(nvar):
+            res = om * other(hs[a]) - mix(us, vs, a) - 0.05 * got[a][2] - wall2 * hs[a]
+            news.append(first[k, a] + step * res)
+        return news
+
+    def edges_of(mc):
+        return mp1 * xp(mc, 1), mm1 * xm(mc, 1)
+
+    def gx(v):
+        return 0.5 * (mp1 * xp(v, 1) - mm1 * xm(v, 1))
+
+    def gy(v):
+        return 0.5 * (yp(v, 1) - ym(v, 1))
+
+    def advance_mean(acc, step):
         s = [0.5 * (v + other(v)) for v in acc]
-
-        def gx(v):
-            return 0.5 * (mp1 * xp(v, 1) - mm1 * xm(v, 1))
-
-        def gy(v):
-            return 0.5 * (yp(v, 1) - ym(v, 1))
-
         force = (
             zero,
             -gx(s[0]) - gy(s[1]),
@@ -393,53 +391,99 @@
             -gx(s[2]) - gy(s[4]) + (s[3] - s[5]) * inv_r,
             -gx(s[6]) - gy(s[7]) - s[8] * inv_r,
         )
-        means = [mean[a] for a in range(nvar)]
-        got = [pieces(m, mp1, mm1) for m in means]
+        got = [pieces(mean[a], mp1, mm1) for a in range(nvar)]
         us, vs = [g[0] for g in got], [g[1] for g in got]
         for a in range(nvar):
             res = force[a] - mix(us, vs, a) - 0.05 * got[a][2]
             mean[a] = mean0[a] + step * res
-        return 0
-
-    lax.fori_loop(0, 4, section, 0)
+
+    edges = edges_of(mean[1])
+    step = SECTION_RATES[0] * time_step
+
+    def landed(k, accs):
+        before, after = accs
+        for s in range(ns):
+            for a in range(nvar):
+                first[k, a, cells * s : cells * s + cells, :] = recv[k, s, a]
+        om = jnp.broadcast_to(recv[k, 0, nvar, 0:1, :], (nx, LANES))
+        omega[k] = om
+        hs = [first[k, a] for a in range(nvar)]
+        news = advance(k, hs, om, edges, step)
+        for a in range(nvar):
+            state[k, a] = news[a]
+        return products(before, hs), products(after, news)
+
+    def arrive(o, accs):
+        k = flip_by(mh, o)
+        for os in range(ns):
+            in_copy(k, flip(ms, os)).wait_recv()
+        return landed(k, accs)
+
+    before, acc = lax.fori_loop(1, nh, arrive, landed(mh, (empty, empty)))
+    advance_mean(before, step)
+
+    def section(i, acc):
+        step = jnp.where(i == 1, SECTION_RATES[1], SECTION_RATES[2]).astype(F32) * time_step
+        edges = edges_of(mean[1])
+
+        def one(k, after):
+            news = advance(k, [state[k, a] for a in range(nvar)], omega[k], edges, step)
+            for a in range(nvar):
+                state[k, a] = news[a]
+            return products(after, news)
+
+        after = lax.fori_loop(0, nh, one, empty, unroll=2)
+        advance_mean(acc, step)
+        return after
+
+    acc = lax.fori_loop(1, 3, section, acc)
+
+    step = SECTION_RATES[3] * time_step
+    edges = edges_of(mean[1])
+    advance_mean(acc, step)
 
     def join(even, odd):
         return jnp.where(is_real, even, odd)
 
     packs = (mean[4], join(mean[0], mean[1]), join(mean[2], mean[3]))
 
-    def leave(k, _):
-        for s in range(ns):
-            for a in range(nvar):
-                back[k, s, a] = state[k, a, cells * s : cells * s + cells, :]
-            for b in range(3):
-                back[k, s, nvar + b] = packs[b][cells * s : cells * s + cells, :]
-        return 0
-
-    lax.fori_loop(0, nh, leave, 0)
-    home[me] = back[mh, ms]
-
-    def back_copy(d, slot):
+    def back_copy(k, s, slot):
+        d = k * ns + s
         return pltpu.make_async_remote_copy(
-            src_ref=back.at[d // ns, lax.rem(d, ns)],
+            src_ref=back.at[k, s],
             dst_ref=home.at[slot],
             send_sem=bs_sem.at[d],
             recv_sem=br_sem.at[slot],
-            device_id=(d // ns, lax.rem(d, ns)),
+            device_id=(k, s),
             device_id_type=MESH_ID,
         )
 
-    def go_back(o, _):
-        d = lax.rem(me + o, nd)
-        back_copy(d, me).start()
+    def finish(k):
+        news = advance(k, [state[k, a] for a in range(nvar)], omega[k], edges, step)
+        for s in range(ns):
+            for a in range(nvar):
+                back[k, s, a] = news[a][cells * s : cells * s + cells, :]
+            for b in range(3):
+                back[k, s, nvar + b] = packs[b][cells * s : cells * s + cells, :]
+
+    def depart(o, _):
+        k = flip_by(mh, nh - 1 - o)
+        finish(k)
+        for os in range(ns - 1, -1, -1):
+            back_copy(k, flip(ms, os), me).start()
         return 0
+
+    lax.fori_loop(0, nh - 1, depart, 0)
+    finish(mh)
+    for os in range(ns - 1, 0, -1):
+        back_copy(mh, flip(ms, os), me).start()
+    home[me] = back[mh, ms]
 
     def land_back(o, _):
         d = lax.rem(me + o, nd)
-        back_copy(d, d).wait_recv()
+        back_copy(d // ns, lax.rem(d, ns), d).wait_recv()
         return 0
 
-    lax.fori_loop(1, nd, go_back, 0)
     lax.fori_loop(1, nd, land_back, 0)
 
     for grp in range(4):
@@ -466,16 +510,13 @@
 
     def sent(o, _):
         d = lax.rem(me + o, nd)
-        out_copy(d).wait_send()
-        back_copy(d, me).wait_send()
+        out_copy(d // ns, lax.rem(d, ns)).wait_send()
+        back_copy(d // ns, lax.rem(d, ns), me).wait_send()
         return 0
 
-    def sent_mean(o, _):
-        mean_out(lax.rem(ms + o, ns)).wait_send()
-        return 0
-
     lax.fori_loop(1, nd, sent, 0)
-    lax.fori_loop(1, ns, sent_mean, 0)
+    for o in range(1, ns):
+        mean_copy(flip(ms, o), ms).wait_send()
 
 
 def radial_shards(nh, ns, harmonics, mean_flow, freq_index, wall_mask, jacobian_x, jacobian_y):
@@ -483,6 +524,7 @@
     nd, nx = nh * ns, ns * cells
     vmem = pl.BlockSpec(memory_space=pltpu.VMEM)
     smem = pl.BlockSpec(memory_space=pltpu.SMEM)
+    anywhere = pl.BlockSpec(memory_space=pl.ANY)
     dims = (nh, ns, nvar, cells, planes // LANES)
     field = (nx, LANES)
     piece = (cells, LANES)
@@ -492,9 +534,13 @@
             jax.ShapeDtypeStruct(mean_flow.shape, F32),
             jax.ShapeDtypeStruct(harmonics.shape, F32),
         ),
-        in_specs=[vmem, vmem, smem, vmem, smem, smem],
+        in_specs=[anywhere, anywhere, smem, anywhere, smem, smem],
         out_specs=(vmem, vmem),
         scratch_shapes=[
+            pltpu.VMEM(harmonics.shape, F32),
+            pltpu.VMEM(mean_flow.shape, F32),
+            pltpu.VMEM(wall_mask.shape, jnp.int32),
+            pltpu.SemaphoreType.DMA((3,)),
             pltpu.VMEM((4 * ROWS, planes), F32),
             pltpu.VMEM((nd, nvar + 4, *piece), F32),
             pltpu.VMEM((nh, ns, nvar + 1, *piece), F32),

time: 31.2 us -> 30.4 us (0.974)
  Pallas kernels: 27.2 us -> 26.6 us
    pallas_call x1, Pallas kernels: 27.2 us -> 26.6 us  [radial_shards(): pl.pallas_call(functools.partial(radial_kernel, dims), out_shape=(jax.Sha...]
where the time goes in v2:
time: 30.4 us; the launch traced here: 30.2 us
  Pallas kernels  26.6 us (88%)
  local copies, waits for them, and re-layouts  2.24 us (7%)
  between operations  1.29 us (4%)
    pallas_call x1, Pallas kernels, radial_shards(): pl.pallas_call(functools.partial(radial_kernel, dims), out_shape=(jax.Sha...  26.6 us
    unnamed x4, local copies, waits for them, and re-layouts  2.24 us

profile of v2, /device:TPU:0, one launch (start us, length us, event | category | flops | bytes accessed | tf_op | source)
XLA Modules:
  0.0 30.2 jit_solution(15327022464999916883)
XLA Ops:
  1.3 26.6 %shard_map.77 = (f32[5,2,2048]{2,1,0:T(2,128)}, f32[1,2,5,2,2048]{4,3,2,1,0:T(2,128)}) custom-call(f32[1,2,5,2,2048]{4,3,2,1,0:T(2,128)} %h_any.1, f32[5,2,2048]{2,1,0:T(2,128)} %m_any.1, s32[1]{0:T(128)S(6)} %copy.10.f_ref, s32[2,2048]{1,0:T(2,128)} %w_any.1, f32[5,5]{1,0:T(8,128)} %jx_ref.1, f32[5,5]{1,0:T(8,128)} %jy_ref.1), custom_call_target="tpu_custom_call" | custom-call | tf_op jit(solution)/shard_map/pallas_call | solution.py:531
  27.9 0.0 copy-start
  27.9 1.6 %copy.11 = f32[5,2,2048]{2,1,0:T(2,128)} copy(f32[5,2,2048]{2,1,0:T(2,128)} %get-tuple-element.4) | data formatting | bytes 163840
  29.5 0.0 copy-done
  29.5 0.7 %copy.12 = f32[1,2,5,2,2048]{4,3,2,1,0:T(2,128)} copy(f32[1,2,5,2,2048]{4,3,2,1,0:T(2,128)S(1)} %copy-done) | data formatting | bytes 327680
Async XLA Ops:
  27.9 1.6 %copy-start = (f32[1,2,5,2,2048]{4,3,2,1,0:T(2,128)S(1)}, f32[1,2,5,2,2048]{4,3,2,1,0:T(2,128)}, u32[]{:S(2)}) copy-start(f32[1,2,5,2,2048]{4,3,2,1,0:T(2,128)} %get-tuple-element.5) | copy-start | bytes 491524

commit v3 on v2

--- a/solution.py
+++ b/solution.py
@@ -157,14 +157,17 @@
 
 def radial_kernel(
     dims, h_any, m_any, f_ref, w_any, jx_ref, jy_ref, mo_ref, ho_ref,
-    h_ref, m_ref, w_ref, in_sem, rows, send, recv, mrecv, state, first, omega, mean, mean0, back, home,
-    hs_sem, hr_sem, ms_sem, mr_sem, bs_sem, br_sem,
+    h_ref, m_ref, w_ref, in_sem, rows, send, relay, recv, mrecv, state, first, omega, mean, mean0, back, home,
+    hs_sem, hr_sem, zs_sem, zr_sem, ms_sem, mr_sem, bs_sem, br_sem,
 ):
     nh, ns, nvar, cells, tiles = dims
     nd = nh * ns
     mh, ms = lax.axis_index("harm"), lax.axis_index("slab")
     me = mh * ns + ms
     nx = ns * cells
+    nz, nc = nh // 2, 2 * ns
+    mz, mx = mh // 2, lax.rem(mh, 2)
+    mc = mx * ns + ms
 
     barrier = pltpu.get_barrier_semaphore()
 
@@ -185,16 +188,16 @@
             weight *= 2
         return out
 
-    def reach(offset):
-        oh, os = offset
-        return min(oh >> 1, 2) + (oh & 1) + (os >> 1) + 0.3 * (os & 1)
-
-    far_first = sorted(
-        [(oh, os) for oh in range(nh) for os in range(ns) if oh or os], key=reach, reverse=True
-    )
-    for oh, os in far_first:
+    near = [(ox, os) for os in range(ns - 1, -1, -1) for ox in (1, 0) if ox or os]
+    lines = range(nz - 1, 0, -1)
+
+    for z in lines:
         pl.semaphore_signal(
-            barrier, inc=1, device_id=(flip(mh, oh), flip(ms, os)), device_id_type=MESH_ID
+            barrier, inc=1, device_id=(2 * flip(mz, z) + mx, ms), device_id_type=MESH_ID
+        )
+    for ox, os in near:
+        pl.semaphore_signal(
+            barrier, inc=1, device_id=(2 * mz + flip(mx, ox), flip(ms, os)), device_id_type=MESH_ID
         )
     loads = [
         pltpu.make_async_copy(src, dst, in_sem.at[i])
@@ -234,43 +237,44 @@
         for g1 in range(2):
             outs = swap_bit((cols[0][g1], cols[1][g1]), 1, low_bit)
             for g0 in range(2):
-                send[:, block_of(2 * grp + g1), g0, :] = outs[g0]
+                for z in range(nz):
+                    send[z, :, block_of(2 * grp + g1), g0, :] = outs[g0][nc * z : nc * z + nc]
     speed = m_ref[1]
     partial_sum = jnp.sum(jnp.sum(speed * speed, axis=1, keepdims=True), axis=0, keepdims=True)
     rate_own = jnp.full((1, 1), 0.25 * f_ref[0].astype(F32), F32)
-    send[:, nvar, 0, :] = jnp.broadcast_to(rate_own, (nd, LANES))
-    send[:, nvar, 1, :] = jnp.broadcast_to(partial_sum, (nd, LANES))
-
-    recv[mh, ms] = send[me, 0 : nvar + 1]
-    mrecv[ms] = send[me, nvar + 1 : nvar + 4]
-
-    pl.semaphore_wait(barrier, nd - 1)
-
-    def out_copy(kd, sd):
-        d = kd * ns + sd
+    send[:, :, nvar, 0, :] = jnp.broadcast_to(rate_own, (nz, nc, LANES))
+    send[:, :, nvar, 1, :] = jnp.broadcast_to(partial_sum, (nz, nc, LANES))
+
+    for z in range(nz):
+        relay[z, mc] = send[z, mc, 0 : nvar + 1]
+    mrecv[ms] = send[mz, mc, nvar + 1 : nvar + 4]
+
+    pl.semaphore_wait(barrier, nz - 1 + nc - 1)
+
+    def near_copy(px, ps, slot):
+        pc = px * ns + ps
         return pltpu.make_async_remote_copy(
-            src_ref=send.at[d, pl.ds(0, nvar + 1)],
-            dst_ref=recv.at[mh, ms],
-            send_sem=hs_sem.at[d],
-            recv_sem=hr_sem.at[me],
-            device_id=(kd, sd),
+            src_ref=send.at[:, pc, pl.ds(0, nvar + 1)],
+            dst_ref=relay.at[:, slot],
+            send_sem=hs_sem.at[pc],
+            recv_sem=hr_sem.at[slot],
+            device_id=(2 * mz + px, ps),
             device_id_type=MESH_ID,
         )
 
-    def in_copy(kd, sd):
-        d = kd * ns + sd
+    def line_copy(pz, slot):
         return pltpu.make_async_remote_copy(
-            src_ref=send.at[d, pl.ds(0, nvar + 1)],
-            dst_ref=recv.at[kd, sd],
-            send_sem=hs_sem.at[d],
-            recv_sem=hr_sem.at[d],
-            device_id=(kd, sd),
+            src_ref=relay.at[pz],
+            dst_ref=recv.at[slot],
+            send_sem=zs_sem.at[pz],
+            recv_sem=zr_sem.at[slot],
+            device_id=(2 * pz + mx, ms),
             device_id_type=MESH_ID,
         )
 
     def mean_copy(s, slot):
         return pltpu.make_async_remote_copy(
-            src_ref=send.at[mh * ns + s, pl.ds(nvar + 1, 3)],
+            src_ref=send.at[mz, mx * ns + s, pl.ds(nvar + 1, 3)],
             dst_ref=mrecv.at[slot],
             send_sem=ms_sem.at[s],
             recv_sem=mr_sem.at[slot],
@@ -278,11 +282,16 @@
             device_id_type=MESH_ID,
         )
 
-    for oh, os in far_first:
-        out_copy(flip(mh, oh), flip(ms, os)).start()
-        if oh == 1 and os == ns - 1:
-            for o in range(ns - 1, 0, -1):
-                mean_copy(flip(ms, o), ms).start()
+    for ox, os in near:
+        near_copy(flip(mx, ox), flip(ms, os), mc).start()
+    for o in range(ns - 1, 0, -1):
+        mean_copy(flip(ms, o), ms).start()
+    for ox, os in near:
+        px, ps = flip(mx, ox), flip(ms, os)
+        near_copy(px, ps, px * ns + ps).wait_recv()
+    for z in lines:
+        line_copy(flip(mz, z), mz).start()
+    recv[mz] = relay[mz]
 
     lane = lax.broadcasted_iota(jnp.int32, (nx, LANES), 1)
     cell = lax.broadcasted_iota(jnp.int32, (nx, LANES), 0)
@@ -298,7 +307,6 @@
 
     for o in range(1, ns):
         peer = flip(ms, o)
-        in_copy(mh, peer).wait_recv()
         mean_copy(peer, peer).wait_recv()
     packed = []
     for b in range(3):
@@ -311,9 +319,9 @@
     for a, value in enumerate((m0, m1, m2, m3, m4)):
         mean[a] = value
         mean0[a] = value
-    total = recv[mh, 0, nvar, 1:2, :]
+    total = recv[mz, mx * ns, nvar, 1:2, :]
     for s in range(1, ns):
-        total = total + recv[mh, s, nvar, 1:2, :]
+        total = total + recv[mz, mx * ns + s, nvar, 1:2, :]
     count = nx * tiles * LANES
     time_step = jnp.broadcast_to(0.9 / (1.0 + jnp.sqrt(total / count)), (nx, LANES))
     wall2 = 2.0 * wall
@@ -400,12 +408,13 @@
     edges = edges_of(mean[1])
     step = SECTION_RATES[0] * time_step
 
-    def landed(k, accs):
+    def landed(z, x, accs):
+        k = 2 * z + x
         before, after = accs
         for s in range(ns):
             for a in range(nvar):
-                first[k, a, cells * s : cells * s + cells, :] = recv[k, s, a]
-        om = jnp.broadcast_to(recv[k, 0, nvar, 0:1, :], (nx, LANES))
+                first[k, a, cells * s : cells * s + cells, :] = recv[z, x * ns + s, a]
+        om = jnp.broadcast_to(recv[z, x * ns, nvar, 0:1, :], (nx, LANES))
         omega[k] = om
         hs = [first[k, a] for a in range(nvar)]
         news = advance(k, hs, om, edges, step)
@@ -413,13 +422,13 @@
             state[k, a] = news[a]
         return products(before, hs), products(after, news)
 
-    def arrive(o, accs):
-        k = flip_by(mh, o)
-        for os in range(ns):
-            in_copy(k, flip(ms, os)).wait_recv()
-        return landed(k, accs)
-
-    before, acc = lax.fori_loop(1, nh, arrive, landed(mh, (empty, empty)))
+    accs = (empty, empty)
+    for oz in range(nz):
+        z = flip(mz, oz)
+        if oz:
+            line_copy(z, z).wait_recv()
+        accs = lax.fori_loop(0, 2, functools.partial(lambda z, x, accs: landed(z, x, accs), z), accs)
+    before, acc = accs
     advance_mean(before, step)
 
     def section(i, acc):
@@ -510,13 +519,16 @@
 
     def sent(o, _):
         d = lax.rem(me + o, nd)
-        out_copy(d // ns, lax.rem(d, ns)).wait_send()
         back_copy(d // ns, lax.rem(d, ns), me).wait_send()
         return 0
 
     lax.fori_loop(1, nd, sent, 0)
     for o in range(1, ns):
         mean_copy(flip(ms, o), ms).wait_send()
+    for ox, os in near:
+        near_copy(flip(mx, ox), flip(ms, os), mc).wait_send()
+    for z in lines:
+        line_copy(flip(mz, z), mz).wait_send()
 
 
 def radial_shards(nh, ns, harmonics, mean_flow, freq_index, wall_mask, jacobian_x, jacobian_y):
@@ -542,8 +554,9 @@
             pltpu.VMEM(wall_mask.shape, jnp.int32),
             pltpu.SemaphoreType.DMA((3,)),
             pltpu.VMEM((4 * ROWS, planes), F32),
-            pltpu.VMEM((nd, nvar + 4, *piece), F32),
-            pltpu.VMEM((nh, ns, nvar + 1, *piece), F32),
+            pltpu.VMEM((nh // 2, 2 * ns, nvar + 4, *piece), F32),
+            pltpu.VMEM((nh // 2, 2 * ns, nvar + 1, *piece), F32),
+            pltpu.VMEM((nh // 2, 2 * ns, nvar + 1, *piece), F32),
             pltpu.VMEM((ns, 3, *piece), F32),
             pltpu.VMEM((nh, nvar, *field), F32),
             pltpu.VMEM((nh, nvar, *field), F32),
@@ -552,8 +565,10 @@
             pltpu.VMEM((nvar, *field), F32),
             pltpu.VMEM((nh, ns, nvar + 3, *piece), F32),
             pltpu.VMEM((nd, nvar + 3, *piece), F32),
-            pltpu.SemaphoreType.DMA((nd,)),
-            pltpu.SemaphoreType.DMA((nd,)),
+            pltpu.SemaphoreType.DMA((2 * ns,)),
+            pltpu.SemaphoreType.DMA((2 * ns,)),
+            pltpu.SemaphoreType.DMA((nh // 2,)),
+            pltpu.SemaphoreType.DMA((nh // 2,)),
             pltpu.SemaphoreType.DMA((ns,)),
             pltpu.SemaphoreType.DMA((ns,)),
             pltpu.SemaphoreType.DMA((nd,)),

time: 30.4 us -> 31.9 us (1.049)
  Pallas kernels: 26.6 us -> 28.1 us
    pallas_call x1, Pallas kernels: 26.6 us -> 28.1 us  [radial_shards(): pl.pallas_call(functools.partial(radial_kernel, dims), out_shape=(jax.Sha...]
where the time goes in v3:
time: 31.9 us; the launch traced here: 31.6 us
  Pallas kernels  28.1 us (88%)
  local copies, waits for them, and re-layouts  2.24 us (7%)
  between operations  1.29 us (4%)
    pallas_call x1, Pallas kernels, radial_shards(): pl.pallas_call(functools.partial(radial_kernel, dims), out_shape=(jax.Sha...  28.1 us
    unnamed x4, local copies, waits for them, and re-layouts  2.24 us

profile of v3, /device:TPU:0, one launch (start us, length us, event | category | flops | bytes accessed | tf_op | source)
XLA Modules:
  0.0 31.6 jit_solution(11889022465728977388)
XLA Ops:
  1.3 28.1 %shard_map.77 = (f32[5,2,2048]{2,1,0:T(2,128)}, f32[1,2,5,2,2048]{4,3,2,1,0:T(2,128)}) custom-call(f32[1,2,5,2,2048]{4,3,2,1,0:T(2,128)} %h_any.1, f32[5,2,2048]{2,1,0:T(2,128)} %m_any.1, s32[1]{0:T(128)S(6)} %copy.10.f_ref, s32[2,2048]{1,0:T(2,128)} %w_any.1, f32[5,5]{1,0:T(8,128)} %jx_ref.1, f32[5,5]{1,0:T(8,128)} %jy_ref.1), custom_call_target="tpu_custom_call" | custom-call | tf_op jit(solution)/shard_map/pallas_call | solution.py:543
  29.4 0.0 copy-start
  29.4 1.6 %copy.11 = f32[5,2,2048]{2,1,0:T(2,128)} copy(f32[5,2,2048]{2,1,0:T(2,128)} %get-tuple-element.4) | data formatting | bytes 163840
  31.0 0.0 copy-done
  31.0 0.7 %copy.12 = f32[1,2,5,2,2048]{4,3,2,1,0:T(2,128)} copy(f32[1,2,5,2,2048]{4,3,2,1,0:T(2,128)S(1)} %copy-done) | data formatting | bytes 327680
Async XLA Ops:
  29.4 1.6 %copy-start = (f32[1,2,5,2,2048]{4,3,2,1,0:T(2,128)S(1)}, f32[1,2,5,2,2048]{4,3,2,1,0:T(2,128)}, u32[]{:S(2)}) copy-start(f32[1,2,5,2,2048]{4,3,2,1,0:T(2,128)} %get-tuple-element.5) | copy-start | bytes 491524

commit v4 on v2

--- a/solution.py
+++ b/solution.py
@@ -156,8 +156,8 @@
 
 
 def radial_kernel(
-    dims, h_any, m_any, f_ref, w_any, jx_ref, jy_ref, mo_ref, ho_ref,
-    h_ref, m_ref, w_ref, in_sem, rows, send, recv, mrecv, state, first, omega, mean, mean0, back, home,
+    dims, h_any, m_any, f_ref, w_any, jx_ref, jy_ref, home,
+    h_ref, m_ref, w_ref, in_sem, rows, send, recv, mrecv, state, first, omega, mean, mean0, back, own_sem,
     hs_sem, hr_sem, ms_sem, mr_sem, bs_sem, br_sem,
 ):
     nh, ns, nvar, cells, tiles = dims
@@ -432,7 +432,7 @@
                 state[k, a] = news[a]
             return products(after, news)
 
-        after = lax.fori_loop(0, nh, one, empty, unroll=2)
+        after = lax.fori_loop(0, nh, one, empty, unroll=4)
         advance_mean(acc, step)
         return after
 
@@ -477,7 +477,8 @@
     finish(mh)
     for os in range(ns - 1, 0, -1):
         back_copy(mh, flip(ms, os), me).start()
-    home[me] = back[mh, ms]
+    own = pltpu.make_async_copy(back.at[mh, ms], home.at[me], own_sem)
+    own.start()
 
     def land_back(o, _):
         d = lax.rem(me + o, nd)
@@ -485,6 +486,26 @@
         return 0
 
     lax.fori_loop(1, nd, land_back, 0)
+
+    own.wait()
+
+    def sent(o, _):
+        d = lax.rem(me + o, nd)
+        out_copy(d // ns, lax.rem(d, ns)).wait_send()
+        back_copy(d // ns, lax.rem(d, ns), me).wait_send()
+        return 0
+
+    lax.fori_loop(1, nd, sent, 0)
+    for o in range(1, ns):
+        mean_copy(flip(ms, o), ms).wait_send()
+
+
+def gather_kernel(dims, home, mo_ref, ho_ref, rows):
+    nh, ns, nvar, cells, tiles = dims
+    nd = nh * ns
+    lane_all = lax.broadcasted_iota(jnp.int32, (nd, LANES), 1)
+    low_bit = lane_all & 1
+    high_bit = (lane_all >> 2) & 1
 
     for grp in range(4):
         cols = []
@@ -508,16 +529,6 @@
     for a in range(nvar - 1):
         mo_ref[a] = take(2 * nvar + 2 + a)
 
-    def sent(o, _):
-        d = lax.rem(me + o, nd)
-        out_copy(d // ns, lax.rem(d, ns)).wait_send()
-        back_copy(d // ns, lax.rem(d, ns), me).wait_send()
-        return 0
-
-    lax.fori_loop(1, nd, sent, 0)
-    for o in range(1, ns):
-        mean_copy(flip(ms, o), ms).wait_send()
-
 
 def radial_shards(nh, ns, harmonics, mean_flow, freq_index, wall_mask, jacobian_x, jacobian_y):
     nvar, cells, planes = mean_flow.shape
@@ -528,14 +539,11 @@
     dims = (nh, ns, nvar, cells, planes // LANES)
     field = (nx, LANES)
     piece = (cells, LANES)
-    return pl.pallas_call(
+    home = pl.pallas_call(
         functools.partial(radial_kernel, dims),
-        out_shape=(
-            jax.ShapeDtypeStruct(mean_flow.shape, F32),
-            jax.ShapeDtypeStruct(harmonics.shape, F32),
-        ),
+        out_shape=jax.ShapeDtypeStruct((nd, nvar + 3, *piece), F32),
         in_specs=[anywhere, anywhere, smem, anywhere, smem, smem],
-        out_specs=(vmem, vmem),
+        out_specs=anywhere,
         scratch_shapes=[
             pltpu.VMEM(harmonics.shape, F32),
             pltpu.VMEM(mean_flow.shape, F32),
@@ -551,7 +559,7 @@
             pltpu.VMEM((nvar, *field), F32),
             pltpu.VMEM((nvar, *field), F32),
             pltpu.VMEM((nh, ns, nvar + 3, *piece), F32),
-            pltpu.VMEM((nd, nvar + 3, *piece), F32),
+            pltpu.SemaphoreType.DMA,
             pltpu.SemaphoreType.DMA((nd,)),
             pltpu.SemaphoreType.DMA((nd,)),
             pltpu.SemaphoreType.DMA((ns,)),
@@ -561,6 +569,16 @@
         ],
         compiler_params=pltpu.CompilerParams(collective_id=0, has_side_effects=True),
     )(harmonics, mean_flow, freq_index, wall_mask, jacobian_x, jacobian_y)
+    return pl.pallas_call(
+        functools.partial(gather_kernel, dims),
+        out_shape=(
+            jax.ShapeDtypeStruct(mean_flow.shape, F32),
+            jax.ShapeDtypeStruct(harmonics.shape, F32),
+        ),
+        in_specs=[vmem],
+        out_specs=(vmem, vmem),
+        scratch_shapes=[pltpu.VMEM((4 * ROWS, planes), F32)],
+    )(home)
 
 
 def fits_radial(nh, ns, harmonics, mean_flow):

time: 30.4 us -> 28.9 us (0.951)
  local copies, waits for them, and re-layouts: 2.24 us -> 0 us
  Pallas kernels: 26.6 us -> 27.4 us
    unnamed x4 -> x0, local copies, waits for them, and re-layouts: 2.24 us -> none
    pallas_call x1 -> x2, Pallas kernels: 26.6 us -> 27.4 us  [the longest x1 25.3 us: radial_shards(): pl.pallas_call(functools.partial(radial_kernel, dims), out_shape=jax.Shap...]
where the time goes in v4:
time: 28.9 us; the launch traced here: 28.7 us
  Pallas kernels  27.4 us (95%)
  between operations  1.28 us (4%)
    pallas_call x1, Pallas kernels, radial_shards(): pl.pallas_call(functools.partial(radial_kernel, dims), out_shape=jax.Shap...  25.3 us
    pallas_call x1, Pallas kernels, radial_shards(): pl.pallas_call(functools.partial(gather_kernel, dims), out_shape=(jax.Sha...  2.07 us

profile of v4, /device:TPU:0, one launch (start us, length us, event | category | flops | bytes accessed | tf_op | source)
XLA Modules:
  0.0 28.7 jit_solution(15286424365178938232)
XLA Ops:
  1.3 25.3 %shard_map.77.home = f32[32,8,2,128]{3,2,1,0:T(2,128)} custom-call(f32[1,2,5,2,2048]{4,3,2,1,0:T(2,128)} %h_any.1, f32[5,2,2048]{2,1,0:T(2,128)} %m_any.1, s32[1]{0:T(128)S(6)} %copy.8.f_ref, s32[2,2048]{1,0:T(2,128)} %w_any.1, f32[5,5]{1,0:T(8,128)} %jx_ref.1, f32[5,5]{1,0:T(8,128)} %jy_ref.1), custom_call_target="tpu_custom_call" | custom-call | tf_op jit(solution)/shard_map/pallas_call | solution.py:542
  26.6 2.1 %shard_map.78 = (f32[5,2,2048]{2,1,0:T(2,128)}, f32[1,2,5,2,2048]{4,3,2,1,0:T(2,128)}) custom-call(f32[32,8,2,128]{3,2,1,0:T(2,128)} %shard_map.77.home), custom_call_target="tpu_custom_call" | custom-call | tf_op jit(solution)/shard_map/pallas_call | solution.py:572

commit v5 on v4

--- a/solution.py
+++ b/solution.py
@@ -419,7 +419,7 @@
             in_copy(k, flip(ms, os)).wait_recv()
         return landed(k, accs)
 
-    before, acc = lax.fori_loop(1, nh, arrive, landed(mh, (empty, empty)))
+    before, acc = lax.fori_loop(1, nh, arrive, landed(mh, (empty, empty)), unroll=nh - 1)
     advance_mean(before, step)
 
     def section(i, acc):
@@ -432,7 +432,7 @@
                 state[k, a] = news[a]
             return products(after, news)
 
-        after = lax.fori_loop(0, nh, one, empty, unroll=4)
+        after = lax.fori_loop(0, nh, one, empty, unroll=nh)
         advance_mean(acc, step)
         return after
 
@@ -473,7 +473,7 @@
             back_copy(k, flip(ms, os), me).start()
         return 0
 
-    lax.fori_loop(0, nh - 1, depart, 0)
+    lax.fori_loop(0, nh - 1, depart, 0, unroll=nh - 1)
     finish(mh)
     for os in range(ns - 1, 0, -1):
         back_copy(mh, flip(ms, os), me).start()
@@ -500,14 +500,28 @@
         mean_copy(flip(ms, o), ms).wait_send()
 
 
-def gather_kernel(dims, home, mo_ref, ho_ref, rows):
+def gather_kernel(dims, home_any, mo_any, ho_any, home, mo_ref, ho_ref, rows, in_sem, out_sem):
     nh, ns, nvar, cells, tiles = dims
     nd = nh * ns
     lane_all = lax.broadcasted_iota(jnp.int32, (nd, LANES), 1)
     low_bit = lane_all & 1
     high_bit = (lane_all >> 2) & 1
 
+    loads = [
+        pltpu.make_async_copy(
+            home_any.at[:, pl.ds(2 * g, 2)], home.at[:, pl.ds(2 * g, 2)], in_sem.at[g]
+        )
+        for g in range(4)
+    ]
+    stores = []
+    for load in loads:
+        load.start()
+
+    def take(at):
+        return rows[pl.ds(cells * at, cells), :]
+
     for grp in range(4):
+        loads[grp].wait()
         cols = []
         for g1 in range(2):
             cols.append(swap_bit([home[:, 2 * grp + g1, g0, :] for g0 in range(2)], 1, low_bit))
@@ -518,22 +532,31 @@
             rows[ROWS * grp : ROWS * grp + ROWS, LANES * t : LANES * t + LANES] = turned[
                 ROWS * t : ROWS * t + ROWS
             ]
-
-    def take(at):
-        return rows[pl.ds(cells * at, cells), :]
-
-    for a in range(nvar):
-        for c in range(2):
-            ho_ref[0, c, a] = take(2 * a + c)
-    mo_ref[nvar - 1] = take(2 * nvar)
-    for a in range(nvar - 1):
-        mo_ref[a] = take(2 * nvar + 2 + a)
+        for pair in (2 * grp, 2 * grp + 1):
+            for c in range(2):
+                if pair < nvar:
+                    ho_ref[0, c, pair] = take(2 * pair + c)
+                elif pair == nvar:
+                    mo_ref[nvar - 1] = take(2 * pair)
+                    break
+                else:
+                    mo_ref[2 * (pair - nvar - 1) + c] = take(2 * pair + c)
+        if 2 * grp < nvar:
+            count = min(2, nvar - 2 * grp)
+            part_of = (0, slice(None), pl.ds(2 * grp, count))
+            stores.append(
+                pltpu.make_async_copy(ho_ref.at[part_of], ho_any.at[part_of], out_sem.at[grp])
+            )
+            stores[-1].start()
+    stores.append(pltpu.make_async_copy(mo_ref, mo_any, out_sem.at[3]))
+    stores[-1].start()
+    for store in stores:
+        store.wait()
 
 
 def radial_shards(nh, ns, harmonics, mean_flow, freq_index, wall_mask, jacobian_x, jacobian_y):
     nvar, cells, planes = mean_flow.shape
     nd, nx = nh * ns, ns * cells
-    vmem = pl.BlockSpec(memory_space=pltpu.VMEM)
     smem = pl.BlockSpec(memory_space=pltpu.SMEM)
     anywhere = pl.BlockSpec(memory_space=pl.ANY)
     dims = (nh, ns, nvar, cells, planes // LANES)
@@ -575,9 +598,16 @@
             jax.ShapeDtypeStruct(mean_flow.shape, F32),
             jax.ShapeDtypeStruct(harmonics.shape, F32),
         ),
-        in_specs=[vmem],
-        out_specs=(vmem, vmem),
-        scratch_shapes=[pltpu.VMEM((4 * ROWS, planes), F32)],
+        in_specs=[anywhere],
+        out_specs=(anywhere, anywhere),
+        scratch_shapes=[
+            pltpu.VMEM((nd, nvar + 3, *piece), F32),
+            pltpu.VMEM(mean_flow.shape, F32),
+            pltpu.VMEM(harmonics.shape, F32),
+            pltpu.VMEM((4 * ROWS, planes), F32),
+            pltpu.SemaphoreType.DMA((4,)),
+            pltpu.SemaphoreType.DMA((4,)),
+        ],
     )(home)
 
 

time: 28.9 us -> 28.9 us (level)
    pallas_call x1, Pallas kernels: 25.3 us -> 24.8 us  [radial_shards(): pl.pallas_call(functools.partial(radial_kernel, dims), out_shape=jax.Shap...]
    pallas_call x1, Pallas kernels: 2.07 us -> 2.6 us  [radial_shards(): pl.pallas_call(functools.partial(gather_kernel, dims), out_shape=(jax.Sha...]
where the time goes in v5:
time: 28.9 us; the launch traced here: 28.7 us
  Pallas kernels  27.4 us (95%)
  between operations  1.28 us (4%)
    pallas_call x1, Pallas kernels, radial_shards(): pl.pallas_call(functools.partial(radial_kernel, dims), out_shape=jax.Shap...  24.8 us
    pallas_call x1, Pallas kernels, radial_shards(): pl.pallas_call(functools.partial(gather_kernel, dims), out_shape=(jax.Sha...  2.6 us

profile of v5, /device:TPU:0, one launch (start us, length us, event | category | flops | bytes accessed | tf_op | source)
XLA Modules:
  0.0 28.7 jit_solution(8612211475198253495)
XLA Ops:
  1.3 24.8 %shard_map.77.home_any = f32[32,8,2,128]{3,2,1,0:T(2,128)} custom-call(f32[1,2,5,2,2048]{4,3,2,1,0:T(2,128)} %h_any.1, f32[5,2,2048]{2,1,0:T(2,128)} %m_any.1, s32[1]{0:T(128)S(6)} %copy.8.f_ref, s32[2,2048]{1,0:T(2,128)} %w_any.1, f32[5,5]{1,0:T(8,128)} %jx_ref.1, f32[5,5]{1,0:T(8,128)} %jy_ref.1), custom_call_target="tpu_custom_call" | custom-call | tf_op jit(solution)/shard_map/pallas_call | solution.py:565
  26.1 2.6 %shard_map.78 = (f32[5,2,2048]{2,1,0:T(2,128)}, f32[1,2,5,2,2048]{4,3,2,1,0:T(2,128)}) custom-call(f32[32,8,2,128]{3,2,1,0:T(2,128)} %shard_map.77.home_any), custom_call_target="tpu_custom_call" | custom-call | tf_op jit(solution)/shard_map/pallas_call | solution.py:595

commit v6 on v4

--- a/solution.py
+++ b/solution.py
@@ -419,7 +419,7 @@
             in_copy(k, flip(ms, os)).wait_recv()
         return landed(k, accs)
 
-    before, acc = lax.fori_loop(1, nh, arrive, landed(mh, (empty, empty)))
+    before, acc = lax.fori_loop(1, nh, arrive, landed(mh, (empty, empty)), unroll=nh - 1)
     advance_mean(before, step)
 
     def section(i, acc):
@@ -432,7 +432,7 @@
                 state[k, a] = news[a]
             return products(after, news)
 
-        after = lax.fori_loop(0, nh, one, empty, unroll=4)
+        after = lax.fori_loop(0, nh, one, empty, unroll=nh)
         advance_mean(acc, step)
         return after
 
@@ -473,7 +473,7 @@
             back_copy(k, flip(ms, os), me).start()
         return 0
 
-    lax.fori_loop(0, nh - 1, depart, 0)
+    lax.fori_loop(0, nh - 1, depart, 0, unroll=nh - 1)
     finish(mh)
     for os in range(ns - 1, 0, -1):
         back_copy(mh, flip(ms, os), me).start()

time: 28.9 us -> 28.4 us (0.983)
  Pallas kernels: 27.4 us -> 26.9 us
    pallas_call x1, Pallas kernels: 25.3 us -> 24.8 us  [radial_shards(): pl.pallas_call(functools.partial(radial_kernel, dims), out_shape=jax.Shap...]
where the time goes in v6:
time: 28.4 us; the launch traced here: 28.2 us
  Pallas kernels  26.9 us (95%)
  between operations  1.28 us (5%)
    pallas_call x1, Pallas kernels, radial_shards(): pl.pallas_call(functools.partial(radial_kernel, dims), out_shape=jax.Shap...  24.8 us
    pallas_call x1, Pallas kernels, radial_shards(): pl.pallas_call(functools.partial(gather_kernel, dims), out_shape=(jax.Sha...  2.07 us

profile of v6, /device:TPU:0, one launch (start us, length us, event | category | flops | bytes accessed | tf_op | source)
XLA Modules:
  0.0 28.2 jit_solution(10126857298170518375)
XLA Ops:
  1.3 24.8 %shard_map.77.home = f32[32,8,2,128]{3,2,1,0:T(2,128)} custom-call(f32[1,2,5,2,2048]{4,3,2,1,0:T(2,128)} %h_any.1, f32[5,2,2048]{2,1,0:T(2,128)} %m_any.1, s32[1]{0:T(128)S(6)} %copy.8.f_ref, s32[2,2048]{1,0:T(2,128)} %w_any.1, f32[5,5]{1,0:T(8,128)} %jx_ref.1, f32[5,5]{1,0:T(8,128)} %jy_ref.1), custom_call_target="tpu_custom_call" | custom-call | tf_op jit(solution)/shard_map/pallas_call | solution.py:542
  26.1 2.1 %shard_map.78 = (f32[5,2,2048]{2,1,0:T(2,128)}, f32[1,2,5,2,2048]{4,3,2,1,0:T(2,128)}) custom-call(f32[32,8,2,128]{3,2,1,0:T(2,128)} %shard_map.77.home), custom_call_target="tpu_custom_call" | custom-call | tf_op jit(solution)/shard_map/pallas_call | solution.py:572
